TPU v7x, 256 devices: a whole 4x4x8 slice. The times are simulated.
256 devices in a mesh: branch: 64 (over x, z, core), sub: 4 (over y).
Axes of the slice: x: 4, y: 4, z: 8, core: 2. Of those that a mesh axis runs over, the one named last changes fastest.
Arguments:
- vectors: float32 [9216, 16, 128], P(('branch', 'sub')), may hold values from -6 to 6
- leaf_basis: float32 [9216, 64, 128], P(('branch', 'sub')), may hold values from -0.5 to 0.5
- near_index: int32 [9216, 3], P(('branch', 'sub')), may hold values from 0 to 9215, as said below
- near_blocks: float32 [9216, 3, 128, 128], P(('branch', 'sub')), may hold values from -0.3125 to 0.3125
- coupling_index: int32 [9216, 4], P(('branch', 'sub')), may hold values from 0 to 9215, as said below
- coupling_blocks: float32 [9216, 4, 64, 64], P(('branch', 'sub')), may hold values from -0.375 to 0.375
- leaf_transfer: float32 [9216, 64, 64], P(('branch', 'sub')), may hold values from -0.125 to 0.125
- cluster_transfer: float32 [256, 64, 64], P(('branch', 'sub')), may hold values from -0.375 to 0.375
- branch_index: int32 [64, 16], P('branch'), may hold values from 0 to 63, as said below
- branch_blocks: float32 [64, 16, 64, 64], P('branch'), may hold values from -0.1875 to 0.1875
Outputs:
- product: float32 [9216, 16, 128], P(('branch', 'sub'))
Inputs may be any that keep to these rules, and one draw needn't show every extreme that they name: `near_index`: entry 0 of row l is l itself; every entry of row l lies within 36 of l. `coupling_index`: every entry of row l lies within 36 of l. `branch_index`: the entries of a row are distinct and differ from the row's own branch cluster.
All inputs are finite; a program needn't handle non-finite values.
Results may differ from a plain program's by a relative error of at most 0.000067.
Values sent between devices are 32-bit elements; how exact they have to be, the bound alone decides.
A program may use at most 64 MiB of HBM per device.

v0:
```python
import jax
import jax.numpy as jnp
from jax import lax
from jax.sharding import PartitionSpec as P

highest = lax.Precision.HIGHEST


def with_halo(block, sides, width):
    for axis, dim in sides:
        count = lax.axis_size(axis)
        forward = [(i, i + 1) for i in range(count - 1)]
        backward = [(target, source) for source, target in forward]
        low = lax.ppermute(
            lax.slice_in_dim(block, block.shape[dim] - width, None, axis=dim), axis, forward
        )
        high = lax.ppermute(lax.slice_in_dim(block, 0, width, axis=dim), axis, backward)
        block = jnp.concatenate([low, block, high], axis=dim)
    return block


def per_device(
    vectors,
    leaf_basis,
    near_index,
    near_blocks,
    coupling_index,
    coupling_blocks,
    leaf_transfer,
    cluster_transfer,
    branch_index,
    branch_blocks,
):
    leaf_count = vectors.shape[0]
    coeffs = jnp.einsum("lrp,lvp->lvr", leaf_basis, vectors, precision=highest)
    wide_points = with_halo(vectors, ((("branch", "sub"), 0),), leaf_count)
    wide_coeffs = with_halo(coeffs, ((("branch", "sub"), 0),), leaf_count)
    anchor = lax.axis_index(("branch", "sub")) * leaf_count - leaf_count
    near_rows = jnp.take(wide_points, near_index - anchor, axis=0)
    near_part = jnp.einsum("lkpq,lkvq->lvp", near_blocks, near_rows, precision=highest)
    coupled_rows = jnp.take(wide_coeffs, coupling_index - anchor, axis=0)
    leaf_far = jnp.einsum("lkrs,lkvs->lvr", coupling_blocks, coupled_rows, precision=highest)
    cluster = jnp.einsum("crs,cvs->vr", leaf_transfer, coeffs, precision=highest)
    share = jnp.einsum("rt,vt->vr", cluster_transfer[0], cluster, precision=highest)
    branch_node = lax.psum(share, "sub")
    nodes = lax.all_gather(branch_node[None], "branch", axis=0, tiled=True)
    chosen = jnp.take(nodes, branch_index[0], axis=0)
    branch_far = jnp.einsum("krs,kvs->vr", branch_blocks[0], chosen, precision=highest)
    cluster_down = jnp.einsum("rt,vr->vt", cluster_transfer[0], branch_far, precision=highest)
    leaf_total = leaf_far + jnp.einsum(
        "crs,vr->cvs", leaf_transfer, cluster_down, precision=highest
    )
    return near_part + jnp.einsum("lrp,lvr->lvp", leaf_basis, leaf_total, precision=highest)


def solution(mesh):
    in_specs = (
        P(("branch", "sub"), None, None),
        P(("branch", "sub"), None, None),
        P(("branch", "sub"), None),
        P(("branch", "sub"), None, None, None),
        P(("branch", "sub"), None),
        P(("branch", "sub"), None, None, None),
        P(("branch", "sub"), None, None),
        P(("branch", "sub"), None, None),
        P("branch", None),
        P("branch", None, None, None),
    )
    out_specs = P(("branch", "sub"), None, None)
    return jax.shard_map(
        per_device, mesh=mesh, in_specs=in_specs, out_specs=out_specs, check_vma=False
    )
```

profile of v0, /device:TPU:1, one launch (start us, length us, event | category | flops | bytes accessed | tf_op | source)
XLA Modules:
  0.0 115.5 jit_solution(5684814676402167963)
XLA Ops:
  0.0 0.0 copy-start
  0.0 0.0 copy-start.7
  0.0 0.0 copy-start.5
  0.0 0.0 copy-start.6
  0.0 0.0 copy-start.1
  0.0 1.2 %copy-done = f32[36,64,128]{2,1,0:T(8,128)S(1)} copy-done((f32[36,64,128]{2,1,0:T(8,128)S(1)}, f32[36,64,128]{2,1,0:T(8,128)}, u32[]{:S(2)}) %copy-start) | copy-done | bytes 1179672
  1.3 2.9 %fusion.21 = f32[36,16,64]{2,1,0:T(8,128)S(1)} fusion(f32[36,16,128]{2,1,0:T(8,128)} %param.10, f32[36,64,128]{2,1,0:T(8,128)S(1)} %copy-done), kind=kOutput, calls=%fused_computation.41 | convolution fusion | flops 56623104 | bytes 1622016 | tf_op jit(solution)/shard_map/lrp,lvp->lvr/dot_general | solution.py:35
  4.2 0.0 copy-start.2
  4.2 6.2 %collective-permute-start.3 = (f32[36,16,64]{2,1,0:T(8,128)S(1)}, f32[36,16,64]{2,1,0:T(8,128)}, u32[]{:S(2)}, u32[]{:S(2)}) collective-permute-start(f32[36,16,64]{2,1,0:T(8,128)S(1)} %fusion.21), channel_id=1, source_target_pairs={{1,0},{2,1},{3,2},{4,3},{5,4},{6,5},{7,6},{8,7},{9,8},{10,9},{11,1... | collective-permute-start | bytes 442376 | tf_op jit(solution)/shard_map/ppermute | solution.py:17
  10.3 1.9 %collective-permute-start.2 = (f32[36,16,64]{2,1,0:T(8,128)S(1)}, f32[36,16,64]{2,1,0:T(8,128)}, u32[]{:S(2)}, u32[]{:S(2)}) collective-permute-start(f32[36,16,64]{2,1,0:T(8,128)S(1)} %fusion.21), channel_id=1, source_target_pairs={{0,1},{1,2},{2,3},{3,4},{4,5},{5,6},{6,7},{7,8},{8,9},{9,10},{10,1... | collective-permute-start | bytes 442376 | tf_op jit(solution)/shard_map/ppermute | solution.py:14
  12.3 4.9 %collective-permute-start.1 = (f32[36,16,128]{2,1,0:T(8,128)}, f32[36,16,128]{2,1,0:T(8,128)}, u32[]{:S(2)}, u32[]{:S(2)}) collective-permute-start(f32[36,16,128]{2,1,0:T(8,128)} %param.10), channel_id=1, source_target_pairs={{1,0},{2,1},{3,2},{4,3},{5,4},{6,5},{7,6},{8,7},{9,8},{10,9},{11,1... | collective-permute-start | bytes 884744 | tf_op jit(solution)/shard_map/ppermute | solution.py:17
  17.1 1.9 %collective-permute-start = (f32[36,16,128]{2,1,0:T(8,128)}, f32[36,16,128]{2,1,0:T(8,128)}, u32[]{:S(2)}, u32[]{:S(2)}) collective-permute-start(f32[36,16,128]{2,1,0:T(8,128)} %param.10), channel_id=1, source_target_pairs={{0,1},{1,2},{2,3},{3,4},{4,5},{5,6},{6,7},{7,8},{8,9},{9,10},{10,1... | collective-permute-start | bytes 884744 | tf_op jit(solution)/shard_map/ppermute | solution.py:14
  19.1 0.0 copy-done.7
  19.1 0.0 copy-done.5
  19.1 0.0 copy-done.6
  19.2 0.1 copy.21
  19.3 0.1 reshape.54
  19.4 0.1 copy.19
  19.5 0.1 reshape.46
  19.6 0.0 copy-done.1
  19.6 1.0 convolution_bitcast_fusion.2
  20.6 0.0 copy-done.2
  20.6 0.2 convolution_bitcast_fusion.5
  20.8 10.3 %psum.7 = f32[1,16,64]{2,1,0:T(8,128)S(1)} all-reduce(f32[1,16,64]{2,1,0:T(8,128)S(1)} %convolution_bitcast_fusion.5), channel_id=1, replica_groups=mesh['branch'=64,'sub'=4] {'sub'}, use_global_device_ids=true, to_apply=%region_0.1 | all-reduce | flops 1024 | bytes 8192 | tf_op jit(solution)/shard_map/psum | solution.py:45
  31.1 56.7 %all_gather.3 = f32[64,16,64]{2,1,0:T(8,128)S(1)} all-gather(f32[1,16,64]{2,1,0:T(8,128)S(1)} %psum.7), channel_id=1, replica_groups=mesh['branch'=64,'sub'=4] {'branch'}, dimensions={0}, use_global_device_ids=true | all-gather | bytes 266240 | tf_op jit(solution)/shard_map/all_gather | solution.py:46
  87.8 0.6 gather_fusion.2
  88.3 1.6 %convolution_bitcast_fusion.4 = f32[16,64]{1,0:T(8,128)S(1)} fusion(f32[1,16,64,64]{3,2,1,0:T(8,128)} %param.19, f32[16,16,64]{2,1,0:T(8,128)S(1)} %gather_fusion.2, pred[16]{0:T(512)(128)(4,1)S(1)} %compare_and_fusion), kind=kOutput, calls=%fused_computation.12 | convolution fusion | flops 12599296 | bytes 331792 | tf_op jit(solution)/shard_map/krs,kvs->vr/dot_general | solution.py:48
  90.0 0.7 copy.20
  90.7 0.7 copy.18
  91.4 0.1 convolution_bitcast_fusion.3
  91.5 0.0 collective-permute-done.3
  91.5 0.0 collective-permute-done.2
  91.5 1.1 pad_maximum_fusion.1
  92.6 0.0 copy-start.4
  92.7 1.8 %gather_fusion.1 = f32[144,16,64]{2,1,0:T(8,128)} fusion(f32[108,16,64]{2,1,0:T(8,128)S(1)} %pad_maximum_fusion.1, s32[1024]{0:T(1024)S(1)} %pad_clamp_fusion.1), kind=kCustom, calls=%fused_computation.1 | custom fusion | bytes 1180224 | tf_op jit(solution)/shard_map/jit(_take)/gather | solution.py:41
  94.5 0.0 copy-done.4
  94.5 6.7 %fusion.3 = f32[36,16,64]{2,1,0:T(8,128)S(1)} fusion(f32[36,4,64,64]{3,2,1,0:T(8,128)} %param.15, f32[36,4,16,64]{3,2,1,0:T(8,128)} %bitcast.46, pred[36,4]{1,0:T(8,128)(4,1)S(1)} %copy-done.4), kind=kOutput, calls=%fused_computation.8 | convolution fusion | flops 113393664 | bytes 3096720 | tf_op jit(solution)/shard_map/lkrs,lkvs->lvr/dot_general | solution.py:42
  101.2 0.7 fusion.2
  101.9 0.0 collective-permute-done.1
  101.9 0.0 collective-permute-done
  101.9 1.2 %pad_maximum_fusion = f32[108,16,128]{2,1,0:T(8,128)S(1)} fusion(f32[36,16,128]{2,1,0:T(8,128)} %collective-permute-done.1, f32[36,16,128]{2,1,0:T(8,128)} %param.10, f32[36,16,128]{2,1,0:T(8,128)} %collective-permute-done), kind=kLoop, calls=%fused_computation.14 | loop fusion | flops 442368 | bytes 1769472 | tf_op jit(solution)/shard_map/concatenate | solution.py:18
  103.1 0.0 copy-start.3
  103.1 0.7 gather_fusion
  103.8 0.0 copy-done.3
  103.8 9.8 %convolution_bitcast_fusion.1 = f32[36,16,128]{2,1,0:T(8,128)S(1)} fusion(f32[36,3,128,128]{3,2,1,0:T(8,128)} %param.13, f32[36,3,16,128]{3,2,1,0:T(8,128)S(1)} %bitcast.47, pred[36,3]{1,0:T(8,128)(4,1)S(1)} %copy-done.3), kind=kOutput, calls=%fused_computation.9 | convolution fusion | flops 339959808 | bytes 8257644 | tf_op jit(solution)/shard_map/lkpq,lkvq->lvp/dot_general | solution.py:40
  113.6 1.9 %convolution_add_fusion = f32[36,16,128]{2,1,0:T(8,128)} fusion(f32[36,16,128]{2,1,0:T(8,128)S(1)} %convolution_bitcast_fusion.1, f32[36,16,64]{2,1,0:T(8,128)S(1)} %fusion.2, f32[36,64,128]{2,1,0:T(8,128)S(1)} %copy-done), kind=kOutput, calls=%fused_computation.5 | convolution fusion | flops 56696832 | bytes 1916928 | tf_op jit(solution)/shard_map/lrp,lvr->lvp/dot_general | solution.py:53
  (7 shorter events, 0.1 us)
Async XLA Ops:
  0.0 1.3 %copy-start = (f32[36,64,128]{2,1,0:T(8,128)S(1)}, f32[36,64,128]{2,1,0:T(8,128)}, u32[]{:S(2)}) copy-start(f32[36,64,128]{2,1,0:T(8,128)} %param.11) | copy-start | bytes 3538948
  0.0 19.1 %copy-start.7 = (s32[1,16]{1,0:T(1,128)S(1)}, s32[1,16]{1,0:T(1,128)}, u32[]{:S(2)}) copy-start(s32[1,16]{1,0:T(1,128)} %param.18) | copy-start | bytes 196
  0.0 19.1 %copy-start.5 = (s32[36,3]{0,1:T(4,128)S(1)}, s32[36,3]{0,1:T(4,128)}, u32[]{:S(2)}) copy-start(s32[36,3]{0,1:T(4,128)} %param.12) | copy-start | bytes 1300
  0.0 19.1 %copy-start.6 = (s32[36,4]{0,1:T(4,128)S(1)}, s32[36,4]{0,1:T(4,128)}, u32[]{:S(2)}) copy-start(s32[36,4]{0,1:T(4,128)} %param.14) | copy-start | bytes 1732
  0.0 19.6 %copy-start.1 = (f32[36,64,64]{2,1,0:T(8,128)S(1)}, f32[36,64,64]{2,1,0:T(8,128)}, u32[]{:S(2)}) copy-start(f32[36,64,64]{2,1,0:T(8,128)} %param.16) | copy-start | bytes 1769476
  4.2 16.5 %copy-start.2 = (f32[1,64,64]{2,1,0:T(8,128)S(1)}, f32[1,64,64]{2,1,0:T(8,128)}, u32[]{:S(2)}) copy-start(f32[1,64,64]{2,1,0:T(8,128)} %param.17) | copy-start | bytes 49156
  4.2 87.3 %collective-permute-start.3 = (f32[36,16,64]{2,1,0:T(8,128)S(1)}, f32[36,16,64]{2,1,0:T(8,128)}, u32[]{:S(2)}, u32[]{:S(2)}) collective-permute-start(f32[36,16,64]{2,1,0:T(8,128)S(1)} %fusion.21), channel_id=1, source_target_pairs={{1,0},{2,1},{3,2},{4,3},{5,4},{6,5},{7,6},{8,7},{9,8},{10,9},{11,1... | collective-permute-start | bytes 442376 | tf_op jit(solution)/shard_map/ppermute | solution.py:17
  10.3 81.2 %collective-permute-start.2 = (f32[36,16,64]{2,1,0:T(8,128)S(1)}, f32[36,16,64]{2,1,0:T(8,128)}, u32[]{:S(2)}, u32[]{:S(2)}) collective-permute-start(f32[36,16,64]{2,1,0:T(8,128)S(1)} %fusion.21), channel_id=1, source_target_pairs={{0,1},{1,2},{2,3},{3,4},{4,5},{5,6},{6,7},{7,8},{8,9},{9,10},{10,1... | collective-permute-start | bytes 442376 | tf_op jit(solution)/shard_map/ppermute | solution.py:14
  12.3 89.6 %collective-permute-start.1 = (f32[36,16,128]{2,1,0:T(8,128)}, f32[36,16,128]{2,1,0:T(8,128)}, u32[]{:S(2)}, u32[]{:S(2)}) collective-permute-start(f32[36,16,128]{2,1,0:T(8,128)} %param.10), channel_id=1, source_target_pairs={{1,0},{2,1},{3,2},{4,3},{5,4},{6,5},{7,6},{8,7},{9,8},{10,9},{11,1... | collective-permute-start | bytes 884744 | tf_op jit(solution)/shard_map/ppermute | solution.py:17
  17.1 84.7 %collective-permute-start = (f32[36,16,128]{2,1,0:T(8,128)}, f32[36,16,128]{2,1,0:T(8,128)}, u32[]{:S(2)}, u32[]{:S(2)}) collective-permute-start(f32[36,16,128]{2,1,0:T(8,128)} %param.10), channel_id=1, source_target_pairs={{0,1},{1,2},{2,3},{3,4},{4,5},{5,6},{6,7},{7,8},{8,9},{9,10},{10,1... | collective-permute-start | bytes 884744 | tf_op jit(solution)/shard_map/ppermute | solution.py:14
  92.6 1.8 %copy-start.4 = (pred[36,4]{1,0:T(8,128)(4,1)S(1)}, pred[36,4]{1,0:T(8,128)(4,1)}, u32[]{:S(2)}) copy-start(pred[36,4]{1,0:T(8,128)(4,1)} %copy.20) | copy-start | bytes 436
  103.1 0.7 copy-start.3
where the time goes:
time: 116 us; the launch traced here: 115 us
  blocking collectives  67 us (58%)
  matrix products  24.9 us (21%)
  starting transfers between devices  14.9 us (13%)
  local copies, waits for them, and re-layouts  6.18 us (5%)
  other arithmetic  2.37 us (2%)
    all_gather x1, blocking collectives, per_device(): nodes = lax.all_gather(branch_node[None], 'branch', axis=0, tiled=True)  56.7 us
    ppermute x2, starting transfers between devices, with_halo(): lax.ppermute(lax.slice_in_dim(block, 0, width, axis=dim), axis, backward)  11 us
    psum x1, blocking collectives, per_device(): branch_node = lax.psum(share, 'sub')  10.3 us
    dot_general x1, matrix products, per_device(): jnp.einsum('lkpq,lkvq->lvp', near_blocks, near_rows, precision=highest)  9.8 us
    dot_general x1, matrix products, per_device(): jnp.einsum('lkrs,lkvs->lvr', coupling_blocks, coupled_rows, precision=hig...  6.69 us
    ppermute x2, starting transfers between devices, with_halo(): lax.ppermute(lax.slice_in_dim(block, block.shape[dim] - width, None, axis...  3.85 us
    dot_general x1, matrix products, per_device(): coeffs = jnp.einsum('lrp,lvp->lvr', leaf_basis, vectors, precision=highest)  2.89 us
  transfers between devices with their start and end apart: 4, of which 0 were waited for; matrix products, arithmetic and copies ran while one was open for 14% of the time, Pallas kernels for 0%

commit v1 on v0

--- a/solution.py
+++ b/solution.py
@@ -43,7 +43,10 @@
     cluster = jnp.einsum("crs,cvs->vr", leaf_transfer, coeffs, precision=highest)
     share = jnp.einsum("rt,vt->vr", cluster_transfer[0], cluster, precision=highest)
     branch_node = lax.psum(share, "sub")
-    nodes = lax.all_gather(branch_node[None], "branch", axis=0, tiled=True)
+    nodes = jnp.concatenate(
+        lax.all_to_all(jnp.stack([branch_node[None]] * lax.axis_size("branch")), "branch", 0, 0),
+        axis=0,
+    )
     chosen = jnp.take(nodes, branch_index[0], axis=0)
     branch_far = jnp.einsum("krs,kvs->vr", branch_blocks[0], chosen, precision=highest)
     cluster_down = jnp.einsum("rt,vr->vt", cluster_transfer[0], branch_far, precision=highest)

time: 116 us -> 82.1 us (0.71)
  blocking collectives: 67 us -> 10.3 us
  starting transfers between devices: 14.9 us -> 29.5 us
  local copies, waits for them, and re-layouts: 6.18 us -> 10.9 us
  other arithmetic: 2.37 us -> 5.7 us
    all_gather x1 -> x0, blocking collectives: 56.7 us -> none  [per_device(): nodes = lax.all_gather(branch_node[None], 'branch', axis=0, tiled=True)]
    all_to_all x0 -> x1, starting transfers between devices: none -> 14.7 us  [per_device(): lax.all_to_all(jnp.stack([branch_node[None]] * lax.axis_size('branch')),...]
    unnamed x16 -> x20, local copies, waits for them, and re-layouts: 1.27 us -> 3.98 us
    all_to_all x0 -> x1, other arithmetic: none -> 2.22 us  [per_device(): lax.all_to_all(jnp.stack([branch_node[None]] * lax.axis_size('branch')),...]
  transfers between devices with their start and end apart: 4 -> 5, of which waited for: 0 -> 0; matrix products, arithmetic and copies ran while one was open for 14% -> 33% of each run, Pallas kernels for 0% -> 0%
where the time goes in v1:
time: 82.1 us; the launch traced here: 81.6 us
  starting transfers between devices  29.5 us (36%)
  matrix products  24.8 us (30%)
  local copies, waits for them, and re-layouts  10.9 us (13%)
  blocking collectives  10.3 us (13%)
  other arithmetic  5.7 us (7%)
    all_to_all x1, starting transfers between devices, per_device(): lax.all_to_all(jnp.stack([branch_node[None]] * lax.axis_size('branch')),...  14.7 us
    ppermute x2, starting transfers between devices, with_halo(): lax.ppermute(lax.slice_in_dim(block, 0, width, axis=dim), axis, backward)  11 us
    psum x1, blocking collectives, per_device(): branch_node = lax.psum(share, 'sub')  10.3 us
    dot_general x1, matrix products, per_device(): jnp.einsum('lkpq,lkvq->lvp', near_blocks, near_rows, precision=highest)  9.77 us
    dot_general x1, matrix products, per_device(): jnp.einsum('lkrs,lkvs->lvr', coupling_blocks, coupled_rows, precision=hig...  6.7 us
    unnamed x20, local copies, waits for them, and re-layouts  3.98 us
    ppermute x2, starting transfers between devices, with_halo(): lax.ppermute(lax.slice_in_dim(block, block.shape[dim] - width, None, axis...  3.85 us
    dot_general x1, matrix products, per_device(): coeffs = jnp.einsum('lrp,lvp->lvr', leaf_basis, vectors, precision=highest)  2.89 us
  transfers between devices with their start and end apart: 5, of which 0 were waited for; matrix products, arithmetic and copies ran while one was open for 33% of the time, Pallas kernels for 0%

profile of v1, /device:TPU:1, one launch (start us, length us, event | category | flops | bytes accessed | tf_op | source)
XLA Modules:
  0.0 81.6 jit_solution(13903362835455736145)
XLA Ops:
  0.0 0.0 copy-start
  0.0 1.3 %copy-done = f32[36,64,128]{2,1,0:T(8,128)S(1)} copy-done((f32[36,64,128]{2,1,0:T(8,128)S(1)}, f32[36,64,128]{2,1,0:T(8,128)}, u32[]{:S(2)}) %copy-start) | copy-done | bytes 1179672
  1.3 2.9 %fusion.22 = f32[36,16,64]{2,1,0:T(8,128)S(1)} fusion(f32[36,16,128]{2,1,0:T(8,128)} %param.10, f32[36,64,128]{2,1,0:T(8,128)S(1)} %copy-done), kind=kOutput, calls=%fused_computation.41 | convolution fusion | flops 56623104 | bytes 1622016 | tf_op jit(solution)/shard_map/lrp,lvp->lvr/dot_general | solution.py:35
  4.2 6.2 %collective-permute-start.3 = (f32[36,16,64]{2,1,0:T(8,128)S(1)}, f32[36,16,64]{2,1,0:T(8,128)S(1)}, u32[]{:S(2)}, u32[]{:S(2)}) collective-permute-start(f32[36,16,64]{2,1,0:T(8,128)S(1)} %fusion.22), channel_id=1, source_target_pairs={{1,0},{2,1},{3,2},{4,3},{5,4},{6,5},{7,6},{8,7},{9,8},{10,9},{11,1... | collective-permute-start | bytes 442376 | tf_op jit(solution)/shard_map/ppermute | solution.py:17
  10.3 1.9 %collective-permute-start.2 = (f32[36,16,64]{2,1,0:T(8,128)S(1)}, f32[36,16,64]{2,1,0:T(8,128)}, u32[]{:S(2)}, u32[]{:S(2)}) collective-permute-start(f32[36,16,64]{2,1,0:T(8,128)S(1)} %fusion.22), channel_id=1, source_target_pairs={{0,1},{1,2},{2,3},{3,4},{4,5},{5,6},{6,7},{7,8},{8,9},{9,10},{10,1... | collective-permute-start | bytes 442376 | tf_op jit(solution)/shard_map/ppermute | solution.py:14
  12.3 4.9 %collective-permute-start.1 = (f32[36,16,128]{2,1,0:T(8,128)}, f32[36,16,128]{2,1,0:T(8,128)}, u32[]{:S(2)}, u32[]{:S(2)}) collective-permute-start(f32[36,16,128]{2,1,0:T(8,128)} %param.10), channel_id=1, source_target_pairs={{1,0},{2,1},{3,2},{4,3},{5,4},{6,5},{7,6},{8,7},{9,8},{10,9},{11,1... | collective-permute-start | bytes 884744 | tf_op jit(solution)/shard_map/ppermute | solution.py:17
  17.1 1.9 %collective-permute-start = (f32[36,16,128]{2,1,0:T(8,128)}, f32[36,16,128]{2,1,0:T(8,128)}, u32[]{:S(2)}, u32[]{:S(2)}) collective-permute-start(f32[36,16,128]{2,1,0:T(8,128)} %param.10), channel_id=1, source_target_pairs={{0,1},{1,2},{2,3},{3,4},{4,5},{5,6},{6,7},{7,8},{8,9},{9,10},{10,1... | collective-permute-start | bytes 884744 | tf_op jit(solution)/shard_map/ppermute | solution.py:14
  19.1 0.0 copy-done.1
  19.1 1.0 %convolution_bitcast_fusion.2 = f32[16,64]{1,0:T(8,128)S(1)} fusion(f32[36,16,64]{2,1,0:T(8,128)S(1)} %fusion.22, f32[36,64,64]{2,1,0:T(8,128)S(1)} %copy-done.1), kind=kOutput, calls=%fused_computation.10 | convolution fusion | flops 28311552 | bytes 741376 | tf_op jit(solution)/shard_map/crs,cvs->vr/dot_general | solution.py:43
  20.1 0.0 copy-done.3
  20.1 0.0 copy-start.8
  20.1 0.0 copy-start.5
  20.1 0.0 copy-start.6
  20.1 0.1 fusion.16
  20.3 10.3 %psum.7 = f32[16,64]{1,0:T(8,128)S(1)} all-reduce(f32[16,64]{1,0:T(8,128)S(1)} %fusion.16), channel_id=1, replica_groups=mesh['branch'=64,'sub'=4] {'sub'}, use_global_device_ids=true, to_apply=%region_0.1 | all-reduce | flops 1024 | bytes 8192 | tf_op jit(solution)/shard_map/psum | solution.py:45
  30.6 1.0 %reshape.83 = f32[64,1,1024]{2,1,0:T(1,128)} reshape(f32[64,1,16,64]{3,2,1,0:T(8,128)S(1)} %stack.3) | data formatting | bytes 524288
  31.6 14.7 %all-to-all-start = ((f32[64,1,1024]{2,1,0:T(1,128)}), f32[64,1,1024]{2,1,0:T(1,128)}, u32[]{:S(2)}, u32[]{:S(2)}) async-start(f32[64,1,1024]{2,1,0:T(1,128)} %reshape.83), calls=%async_computation | async-start | bytes 524288 | tf_op jit(solution)/shard_map/all_to_all | solution.py:47
  46.4 0.5 compare_and_fusion
  46.9 0.0 copy-done.6
  46.9 0.6 pad_clamp_fusion
  47.5 0.1 copy.17
  47.6 0.1 reshape.60
  47.8 0.7 copy.16
  48.5 0.1 copy.14
  48.6 0.1 copy.15
  48.7 0.1 reshape.52
  48.8 0.0 collective-permute-done.3
  48.8 0.0 copy-start.2
  48.8 0.7 copy-done.2
  49.5 0.0 collective-permute-done.2
  49.5 1.1 %pad_maximum_fusion.1 = f32[108,16,64]{2,1,0:T(8,128)S(1)} fusion(f32[36,16,64]{2,1,0:T(8,128)} %copy-done.2, f32[36,16,64]{2,1,0:T(8,128)S(1)} %fusion.22, f32[36,16,64]{2,1,0:T(8,128)} %collective-permute-done.2), kind=kLoop, calls=%fused_computation.14 | loop fusion | flops 221184 | bytes 884736 | tf_op jit(solution)/shard_map/concatenate | solution.py:18
  50.7 1.8 %gather_fusion.1 = f32[144,16,64]{2,1,0:T(8,128)} fusion(f32[108,16,64]{2,1,0:T(8,128)S(1)} %pad_maximum_fusion.1, s32[1024]{0:T(1024)S(1)} %pad_clamp_fusion.1), kind=kCustom, calls=%fused_computation.1 | custom fusion | bytes 1180224 | tf_op jit(solution)/shard_map/jit(_take)/gather | solution.py:41
  52.5 6.7 %fusion.3 = f32[36,16,64]{2,1,0:T(8,128)S(1)} fusion(f32[36,4,64,64]{3,2,1,0:T(8,128)} %param.15, f32[36,4,16,64]{3,2,1,0:T(8,128)} %bitcast.45, pred[36,4]{1,0:T(8,128)(4,1)} %copy.16), kind=kOutput, calls=%fused_computation.8 | convolution fusion | flops 113393664 | bytes 3096720 | tf_op jit(solution)/shard_map/lkrs,lkvs->lvr/dot_general | solution.py:42
  59.2 0.0 collective-permute-done.1
  59.2 0.0 collective-permute-done
  59.2 1.2 %pad_maximum_fusion = f32[108,16,128]{2,1,0:T(8,128)S(1)} fusion(f32[36,16,128]{2,1,0:T(8,128)} %collective-permute-done.1, f32[36,16,128]{2,1,0:T(8,128)} %param.10, f32[36,16,128]{2,1,0:T(8,128)} %collective-permute-done), kind=kLoop, calls=%fused_computation.13 | loop fusion | flops 442368 | bytes 1769472 | tf_op jit(solution)/shard_map/concatenate | solution.py:18
  60.4 1.6 %gather_fusion = f32[108,16,128]{2,1,0:T(8,128)} fusion(f32[108,16,128]{2,1,0:T(8,128)S(1)} %pad_maximum_fusion, s32[1024]{0:T(1024)S(1)} %pad_clamp_fusion.2), kind=kCustom, calls=%fused_computation | custom fusion | bytes 1769904 | tf_op jit(solution)/shard_map/jit(_take)/gather | solution.py:39
  62.0 9.8 %convolution_bitcast_fusion.1 = f32[36,16,128]{2,1,0:T(8,128)S(1)} fusion(f32[36,3,128,128]{3,2,1,0:T(8,128)} %param.13, f32[36,3,16,128]{3,2,1,0:T(8,128)} %bitcast.46, pred[36,3]{1,0:T(8,128)(4,1)S(1)} %copy.14), kind=kOutput, calls=%fused_computation.9 | convolution fusion | flops 339959808 | bytes 8257644 | tf_op jit(solution)/shard_map/lkpq,lkvq->lvp/dot_general | solution.py:40
  71.8 0.0 copy-start.4
  71.8 0.0 all-to-all-done
  71.9 0.5 broadcast.52
  72.4 2.2 %reduce = f32[64,1024]{1,0:T(8,128)S(1)} reduce(f32[64,1,1024]{2,1,0:T(1,128)} %all-to-all-done, f32[]{:T(128)} %broadcast.52), dimensions={1}, to_apply=%all_to_all.3.reduce_sub_computation | reduce | bytes 524292 | tf_op jit(solution)/shard_map/all_to_all | solution.py:47
  74.6 0.9 %reshape.84 = f32[64,1,16,64]{3,2,1,0:T(8,128)} reshape(f32[64,1024]{1,0:T(8,128)S(1)} %reduce) | data formatting | bytes 524288
  75.5 1.7 %gather_fusion.2 = f32[16,16,64]{2,1,0:T(8,128)S(1)} fusion(f32[64,16,64]{2,1,0:T(8,128)} %bitcast.47, s32[1024]{0:T(1024)} %pad_clamp_fusion), kind=kCustom, calls=%fused_computation.2 | custom fusion | bytes 131136 | tf_op jit(solution)/shard_map/jit(_take)/gather | solution.py:50
  77.3 1.6 %convolution_bitcast_fusion.4 = f32[16,64]{1,0:T(8,128)S(1)} fusion(f32[1,16,64,64]{3,2,1,0:T(8,128)} %param.19, f32[16,16,64]{2,1,0:T(8,128)S(1)} %gather_fusion.2, pred[16]{0:T(512)(128)(4,1)S(1)} %copy-done.7), kind=kOutput, calls=%fused_computation.12 | convolution fusion | flops 12599296 | bytes 331792 | tf_op jit(solution)/shard_map/krs,kvs->vr/dot_general | solution.py:51
  78.9 0.1 convolution_bitcast_fusion.3
  79.0 0.7 fusion.2
  79.7 1.8 %convolution_add_fusion = f32[36,16,128]{2,1,0:T(8,128)} fusion(f32[36,16,128]{2,1,0:T(8,128)S(1)} %convolution_bitcast_fusion.1, f32[36,16,64]{2,1,0:T(8,128)S(1)} %fusion.2, f32[36,64,128]{2,1,0:T(8,128)S(1)} %copy-done), kind=kOutput, calls=%fused_computation.5 | convolution fusion | flops 56696832 | bytes 1916928 | tf_op jit(solution)/shard_map/lrp,lvr->lvp/dot_general | solution.py:56
  (13 shorter events, 0.1 us)
Async XLA Ops:
  0.0 1.3 %copy-start = (f32[36,64,128]{2,1,0:T(8,128)S(1)}, f32[36,64,128]{2,1,0:T(8,128)}, u32[]{:S(2)}) copy-start(f32[36,64,128]{2,1,0:T(8,128)} %param.11) | copy-start | bytes 3538948
  0.0 19.1 %copy-start.1 = (f32[36,64,64]{2,1,0:T(8,128)S(1)}, f32[36,64,64]{2,1,0:T(8,128)}, u32[]{:S(2)}) copy-start(f32[36,64,64]{2,1,0:T(8,128)} %param.16) | copy-start | bytes 1769476
  4.2 15.9 %copy-start.3 = (f32[1,64,64]{2,1,0:T(8,128)S(1)}, f32[1,64,64]{2,1,0:T(8,128)}, u32[]{:S(2)}) copy-start(f32[1,64,64]{2,1,0:T(8,128)} %param.17) | copy-start | bytes 49156
  4.2 44.6 %collective-permute-start.3 = (f32[36,16,64]{2,1,0:T(8,128)S(1)}, f32[36,16,64]{2,1,0:T(8,128)S(1)}, u32[]{:S(2)}, u32[]{:S(2)}) collective-permute-start(f32[36,16,64]{2,1,0:T(8,128)S(1)} %fusion.22), channel_id=1, source_target_pairs={{1,0},{2,1},{3,2},{4,3},{5,4},{6,5},{7,6},{8,7},{9,8},{10,9},{11,1... | collective-permute-start | bytes 442376 | tf_op jit(solution)/shard_map/ppermute | solution.py:17
  10.3 39.2 %collective-permute-start.2 = (f32[36,16,64]{2,1,0:T(8,128)S(1)}, f32[36,16,64]{2,1,0:T(8,128)}, u32[]{:S(2)}, u32[]{:S(2)}) collective-permute-start(f32[36,16,64]{2,1,0:T(8,128)S(1)} %fusion.22), channel_id=1, source_target_pairs={{0,1},{1,2},{2,3},{3,4},{4,5},{5,6},{6,7},{7,8},{8,9},{9,10},{10,1... | collective-permute-start | bytes 442376 | tf_op jit(solution)/shard_map/ppermute | solution.py:14
  12.3 46.9 %collective-permute-start.1 = (f32[36,16,128]{2,1,0:T(8,128)}, f32[36,16,128]{2,1,0:T(8,128)}, u32[]{:S(2)}, u32[]{:S(2)}) collective-permute-start(f32[36,16,128]{2,1,0:T(8,128)} %param.10), channel_id=1, source_target_pairs={{1,0},{2,1},{3,2},{4,3},{5,4},{6,5},{7,6},{8,7},{9,8},{10,9},{11,1... | collective-permute-start | bytes 884744 | tf_op jit(solution)/shard_map/ppermute | solution.py:17
  17.1 42.1 %collective-permute-start = (f32[36,16,128]{2,1,0:T(8,128)}, f32[36,16,128]{2,1,0:T(8,128)}, u32[]{:S(2)}, u32[]{:S(2)}) collective-permute-start(f32[36,16,128]{2,1,0:T(8,128)} %param.10), channel_id=1, source_target_pairs={{0,1},{1,2},{2,3},{3,4},{4,5},{5,6},{6,7},{7,8},{8,9},{9,10},{10,1... | collective-permute-start | bytes 884744 | tf_op jit(solution)/shard_map/ppermute | solution.py:14
  20.1 26.3 %copy-start.8 = (s32[1,16]{1,0:T(1,128)S(1)}, s32[1,16]{1,0:T(1,128)}, u32[]{:S(2)}) copy-start(s32[1,16]{1,0:T(1,128)} %param.18) | copy-start | bytes 196
  20.1 26.8 %copy-start.5 = (s32[36,3]{0,1:T(4,128)S(1)}, s32[36,3]{0,1:T(4,128)}, u32[]{:S(2)}) copy-start(s32[36,3]{0,1:T(4,128)} %param.12) | copy-start | bytes 1300
  20.1 26.8 %copy-start.6 = (s32[36,4]{0,1:T(4,128)S(1)}, s32[36,4]{0,1:T(4,128)}, u32[]{:S(2)}) copy-start(s32[36,4]{0,1:T(4,128)} %param.14) | copy-start | bytes 1732
  31.6 40.2 %all-to-all-start = ((f32[64,1,1024]{2,1,0:T(1,128)}), f32[64,1,1024]{2,1,0:T(1,128)}, u32[]{:S(2)}, u32[]{:S(2)}) async-start(f32[64,1,1024]{2,1,0:T(1,128)} %reshape.83), calls=%async_computation | async-start | bytes 524288 | tf_op jit(solution)/shard_map/all_to_all | solution.py:47
  48.8 0.7 copy-start.2
  71.8 5.4 %copy-start.7 = (pred[16]{0:T(512)(128)(4,1)S(1)}, pred[16]{0:T(512)(128)(4,1)}, u32[]{:S(2)}) copy-start(pred[16]{0:T(512)(128)(4,1)} %compare_and_fusion) | copy-start | bytes 52
  71.8 7.0 %copy-start.4 = (f32[1,64,64]{2,1,0:T(8,128)S(1)}, f32[1,64,64]{2,1,0:T(8,128)}, u32[]{:S(2)}) copy-start(f32[1,64,64]{2,1,0:T(8,128)} %param.17) | copy-start | bytes 49156
